TPU v7x, 128 devices: a whole 4x4x4 slice. The times are simulated.
128 devices in a mesh: alpha: 8 (over x, core), beta: 16 (over z, y).
Axes of the slice: x: 4, y: 4, z: 4, core: 2. Of those that a mesh axis runs over, the one named last changes fastest.
Arguments:
- csf_coef: float32 [42, 98304], P(None, ('alpha', 'beta')), may hold values from -18 to 18
- conf_class: int32 [98304], P(('alpha', 'beta')), may hold values from 0 to 5
- conf_tile: int32 [98304, 1], P(('alpha', 'beta')), may hold values from 0 to 127, as said below
- transforms: float32 [6, 42, 256], replicated, may hold values from -1 to 1
- alpha_targets: int32 [16, 12288], P(None, 'alpha'), may hold values from 0 to 12287, as said below
- alpha_values: bfloat16 [16, 12288], P(None, 'alpha'), may hold values from -1.796875 to 1.796875
- alpha_counts: int32 [12288], P('alpha'), may hold values from 1 to 16, as said below
- beta_targets: int32 [16, 6144], P(None, 'beta'), may hold values from 0 to 6143, as said below
- beta_values: bfloat16 [16, 6144], P(None, 'beta'), may hold values from -1.796875 to 1.796875
- beta_counts: int32 [6144], P('beta'), may hold values from 1 to 16, as said below
- det_diag: float32 [12288, 6144], P('alpha', 'beta'), may hold values from 0.5 to 2
Outputs:
- residual: float32 [42, 98304], P(None, ('alpha', 'beta'))
- residual_rms: float32 [], replicated
Inputs may be any that keep to these rules, and one draw needn't show every extreme that they name: `conf_tile`: among the 768 configurations of one device no tile is named more than 18 times; in every draw some tile is named exactly 18 times by the configurations of every device. `alpha_targets`: in each column the 16 entries are distinct and differ from the column's own string. `beta_targets`: in each column the 16 entries are distinct and differ from the column's own string. `alpha_counts`: some string has exactly 16. `beta_counts`: some string has exactly 16.
All inputs are finite; a program needn't handle non-finite values.
Results may differ from a plain program's by a relative error of at most 0.00075.
The roundings to bfloat16 on the way count: a program that leaves them out, or rounds other values in their place, can miss the bound.
Values may be sent and summed in bfloat16 or wider, within the bound.
No kernel may reach another device: no remote copies, remote signals or barrier semaphores. Data moves between devices by JAX's collectives and lax.ppermute only.
A program may use at most 128 MiB of HBM per device.

v0:
```python
import math
import jax
import jax.numpy as jnp
from jax import lax
from jax.sharding import PartitionSpec as P


def class_forward(coefs, classes, transforms):
    summed = jnp.zeros((coefs.shape[1], transforms.shape[2]), jnp.float32)
    for class_id in range(transforms.shape[0]):
        masked = jnp.where(classes[None, :] == class_id, coefs, jnp.zeros_like(coefs))
        summed = summed + lax.dot_general(
            masked,
            transforms[class_id],
            (((0,), (0,)), ((), ())),
            precision=lax.Precision.HIGHEST,
            preferred_element_type=jnp.float32,
        )
    return summed


def class_backward(values, classes, transforms):
    summed = jnp.zeros((transforms.shape[1], values.shape[0]), jnp.float32)
    for class_id in range(transforms.shape[0]):
        product = lax.dot_general(
            transforms[class_id],
            values,
            (((1,), (1,)), ((), ())),
            precision=lax.Precision.HIGHEST,
            preferred_element_type=jnp.float32,
        )
        summed = summed + jnp.where(classes[None, :] == class_id, product, jnp.zeros_like(product))
    return summed


def bucket_slots(chosen_tiles, buckets):
    onehot = (chosen_tiles[:, None] == jnp.arange(buckets, dtype=jnp.int32)[None, :]).astype(
        jnp.int32
    )
    running = jnp.cumsum(onehot, axis=0) - onehot
    return jnp.sum(onehot * running, axis=1)


def live_weights(values, counts):
    active = jnp.arange(values.shape[0], dtype=jnp.int32)[:, None] < counts[None, :]
    return jnp.where(active, values.astype(jnp.float32), jnp.zeros(values.shape, jnp.float32))


def coupling_block(targets, weights, first_row, block_rows, columns):
    block_targets = lax.dynamic_slice_in_dim(targets, first_row, block_rows, 1)
    block_weights = lax.dynamic_slice_in_dim(weights, first_row, block_rows, 1)
    coupling = jnp.zeros((block_rows, columns.shape[0]), jnp.float32)
    for excitation in range(targets.shape[0]):
        coupling = coupling + jnp.where(
            block_targets[excitation][:, None] == columns[None, :],
            block_weights[excitation][:, None],
            jnp.float32(0.0),
        )
    return coupling.astype(jnp.bfloat16)


def alpha_fold(targets, weights, block_rows, summed, gathered):
    columns = jnp.arange(gathered.shape[0], dtype=jnp.int32)

    def alpha_one_block(block_id):
        coupling = coupling_block(targets, weights, block_id * block_rows, block_rows, columns)
        return jnp.dot(coupling, gathered, preferred_element_type=jnp.float32)

    blocks = lax.map(alpha_one_block, jnp.arange(summed.shape[0] // block_rows, dtype=jnp.int32))
    return blocks.reshape(summed.shape)


def beta_fold(targets, weights, block_rows, summed, gathered):
    columns = jnp.arange(gathered.shape[1], dtype=jnp.int32)

    def beta_one_block(block_id):
        coupling = coupling_block(targets, weights, block_id * block_rows, block_rows, columns)
        return lax.dot_general(
            gathered, coupling, (((1,), (1,)), ((), ())), preferred_element_type=jnp.float32
        )

    blocks = lax.map(beta_one_block, jnp.arange(summed.shape[1] // block_rows, dtype=jnp.int32))
    return jnp.moveaxis(blocks, 0, 1).reshape(summed.shape)


def body(
    csf_coef,
    conf_class,
    conf_tile,
    transforms,
    alpha_targets,
    alpha_values,
    alpha_counts,
    beta_targets,
    beta_values,
    beta_counts,
    det_diag,
):
    nalpha = lax.axis_size("alpha")
    beta_devices = lax.axis_size("beta")
    devices = nalpha * beta_devices
    local_confs = csf_coef.shape[1]
    capacity = 3 * local_confs // devices
    rows_alpha, cols_beta = det_diag.shape
    det_width = transforms.shape[2]
    target_tile = conf_tile[:, 0]
    slot_index = bucket_slots(target_tile, devices)
    det_values = class_forward(csf_coef, conf_class, transforms).astype(jnp.bfloat16)
    outgoing = (
        jnp.zeros((devices, capacity, det_width), jnp.bfloat16)
        .at[target_tile, slot_index]
        .set(det_values)
    )
    arrived = lax.all_to_all(outgoing, ("alpha", "beta"), split_axis=0, concat_axis=0, tiled=True)
    amplitude = arrived.reshape(rows_alpha, cols_beta)
    alpha_weights = live_weights(alpha_values, alpha_counts)
    alpha_term = alpha_fold(
        alpha_targets,
        alpha_weights,
        math.gcd(rows_alpha, 256),
        jnp.zeros((rows_alpha, cols_beta), jnp.float32),
        lax.all_gather(amplitude, "alpha", axis=0, tiled=True),
    )
    beta_weights = live_weights(beta_values, beta_counts)
    beta_term = beta_fold(
        beta_targets,
        beta_weights,
        math.gcd(cols_beta, 256),
        jnp.zeros((rows_alpha, cols_beta), jnp.float32),
        lax.all_gather(amplitude, "beta", axis=1, tiled=True),
    )
    sigma_grid = (alpha_term + beta_term + det_diag * amplitude.astype(jnp.float32)).astype(
        jnp.bfloat16
    )
    returned = lax.all_to_all(
        sigma_grid.reshape(devices, capacity, det_width),
        ("alpha", "beta"),
        split_axis=0,
        concat_axis=0,
        tiled=True,
    )
    sigma_dets = returned[target_tile, slot_index].astype(jnp.float32)
    sigma_csf = class_backward(sigma_dets, conf_class, transforms)
    own_square = jnp.sum(csf_coef * csf_coef)
    own_cross = jnp.sum(csf_coef * sigma_csf)
    total_entries = csf_coef.shape[0] * local_confs * devices
    square_sum, cross_sum = lax.psum((own_square, own_cross), ("alpha", "beta"))
    rayleigh = cross_sum / square_sum
    residual = sigma_csf - rayleigh * csf_coef
    residual_square = lax.psum(jnp.sum(residual * residual), ("alpha", "beta"))
    residual_rms = jnp.sqrt(residual_square / total_entries)
    return (residual, residual_rms)


def solution(mesh):
    placed = (
        P(None, ("alpha", "beta")),
        P(("alpha", "beta")),
        P(("alpha", "beta"), None),
        P(),
        P(None, "alpha"),
        P(None, "alpha"),
        P("alpha"),
        P(None, "beta"),
        P(None, "beta"),
        P("beta"),
        P("alpha", "beta"),
    )
    return jax.shard_map(
        body,
        mesh=mesh,
        in_specs=placed,
        out_specs=(P(None, ("alpha", "beta")), P()),
        check_vma=False,
    )
```

profile of v0, /device:TPU:1, one launch (start us, length us, event | category | flops | bytes accessed | tf_op | source)
XLA Modules:
  0.0 629.4 jit_solution(12536454217057345708)
XLA Ops:
  9.5 1.3 fusion.143
  10.8 1.6 fusion.97
  16.9 37.6 %scatter_fusion = bf16[128,18,256]{2,0,1:T(8,128)(2,1)S(1)} fusion(bf16[128,18,256]{2,0,1:T(8,128)(2,1)S(1)} %broadcast_in_dim.410, s32[768]{0:T(1024)S(1)} %get-tuple-element.263, bf16[768,256]{1,0:T(8,128)(2,1)S(1)} %fusion.80), kind=kCustom, calls=%fused_computation.1 | custom fusion | bytes 1185792 | tf_op jit(solution)/shard_map/scatter | solution.py:112
  55.2 35.2 %all_to_all.10 = bf16[128,18,256]{2,1,0:T(8,128)(2,1)S(1)} all-to-all(bf16[128,18,256]{2,1,0:T(8,128)(2,1)S(1)} %copy.27), channel_id=1, replica_groups=mesh['alpha'=8,'beta'=16] {'alpha','beta'}, dimensions={0} | all-to-all | bytes 2359296 | tf_op jit(solution)/shard_map/all_to_all | solution.py:114
  90.4 1.7 reshape.130
  93.5 49.5 %all-gather.3.cloned.1.call-done = bf16[12288,384]{1,0:T(8,128)(2,1)} async-done(((bf16[1536,384]{1,0:T(8,128)(2,1)}), bf16[12288,384]{1,0:T(8,128)(2,1)}) %all-gather.3.cloned.1.call-update) | async-done | bytes 9437200 | tf_op jit(solution)/shard_map/all_gather | solution.py:122
  143.1 233.3 %while.24 = (s32[]{:T(128)}, f32[6,256,384]{2,1,0:T(8,128)}, s32[6]{0:T(128)S(1)}, s32[16,1536]{1,0:T(8,128)}, f32[16,1536]{1,0:T(8,128)S(1)}, /*index=5*/bf16[1...) while((s32[]{:T(128)}, f32[6,256,384]{2,1,0:T(8,128)}, ...), condition=%wide.region_5.6_spmd.clone.clone, body=%wide.region_4.5_spmd.clone.clone.sunk | while | flops 2566914048 | bytes 9929803 | solution.py:69
  163.5 1.4 constant_dynamic-slice_fusion.7
  164.9 31.6 %fusion.159 = f32[6,256,384]{2,1,0:T(8,128)} fusion(f32[6,256,384]{2,1,0:T(8,128)} %get-tuple-element.666, s32[]{:T(128)} %get-tuple-element.665, bf16[12288,384]{1,0:T(8,128)(2,1)} %get-tuple-element.695, f32[256]{0:T(256)S(1)} %bitcast.268, s32[256]{0:T(256)S(1)} %bitcast.284, f32[256]{0:T(256)S(1)} %bitcast.254, s32[256]{0:T(256)S(1)} %bitcast.270, ...), kind=kOutput, calls=%fused_computation.56.clone.1 | convolution fusion | flops 2566914048 | bytes 9863680 | tf_op jit(solution)/shard_map/while/body/eval_jaxpr/dot_general | solution.py:67
  198.0 1.4 constant_dynamic-slice_fusion.7
  199.4 31.8 %fusion.159 = f32[6,256,384]{2,1,0:T(8,128)} fusion(f32[6,256,384]{2,1,0:T(8,128)} %get-tuple-element.666, s32[]{:T(128)} %get-tuple-element.665, bf16[12288,384]{1,0:T(8,128)(2,1)} %get-tuple-element.695, f32[256]{0:T(256)S(1)} %bitcast.268, s32[256]{0:T(256)S(1)} %bitcast.284, f32[256]{0:T(256)S(1)} %bitcast.254, s32[256]{0:T(256)S(1)} %bitcast.270, ...), kind=kOutput, calls=%fused_computation.56.clone.1 | convolution fusion | flops 2566914048 | bytes 9863680 | tf_op jit(solution)/shard_map/while/body/eval_jaxpr/dot_general | solution.py:67
  232.6 1.4 constant_dynamic-slice_fusion.7
  234.0 31.4 %fusion.159 = f32[6,256,384]{2,1,0:T(8,128)} fusion(f32[6,256,384]{2,1,0:T(8,128)} %get-tuple-element.666, s32[]{:T(128)} %get-tuple-element.665, bf16[12288,384]{1,0:T(8,128)(2,1)} %get-tuple-element.695, f32[256]{0:T(256)S(1)} %bitcast.268, s32[256]{0:T(256)S(1)} %bitcast.284, f32[256]{0:T(256)S(1)} %bitcast.254, s32[256]{0:T(256)S(1)} %bitcast.270, ...), kind=kOutput, calls=%fused_computation.56.clone.1 | convolution fusion | flops 2566914048 | bytes 9863680 | tf_op jit(solution)/shard_map/while/body/eval_jaxpr/dot_general | solution.py:67
  267.0 1.4 constant_dynamic-slice_fusion.7
  268.4 31.4 %fusion.159 = f32[6,256,384]{2,1,0:T(8,128)} fusion(f32[6,256,384]{2,1,0:T(8,128)} %get-tuple-element.666, s32[]{:T(128)} %get-tuple-element.665, bf16[12288,384]{1,0:T(8,128)(2,1)} %get-tuple-element.695, f32[256]{0:T(256)S(1)} %bitcast.268, s32[256]{0:T(256)S(1)} %bitcast.284, f32[256]{0:T(256)S(1)} %bitcast.254, s32[256]{0:T(256)S(1)} %bitcast.270, ...), kind=kOutput, calls=%fused_computation.56.clone.1 | convolution fusion | flops 2566914048 | bytes 9863680 | tf_op jit(solution)/shard_map/while/body/eval_jaxpr/dot_general | solution.py:67
  301.3 1.2 constant_dynamic-slice_fusion.7
  302.5 31.5 %fusion.159 = f32[6,256,384]{2,1,0:T(8,128)} fusion(f32[6,256,384]{2,1,0:T(8,128)} %get-tuple-element.666, s32[]{:T(128)} %get-tuple-element.665, bf16[12288,384]{1,0:T(8,128)(2,1)} %get-tuple-element.695, f32[256]{0:T(256)S(1)} %bitcast.268, s32[256]{0:T(256)S(1)} %bitcast.284, f32[256]{0:T(256)S(1)} %bitcast.254, s32[256]{0:T(256)S(1)} %bitcast.270, ...), kind=kOutput, calls=%fused_computation.56.clone.1 | convolution fusion | flops 2566914048 | bytes 9863680 | tf_op jit(solution)/shard_map/while/body/eval_jaxpr/dot_general | solution.py:67
  335.4 1.2 constant_dynamic-slice_fusion.7
  336.6 31.4 %fusion.159 = f32[6,256,384]{2,1,0:T(8,128)} fusion(f32[6,256,384]{2,1,0:T(8,128)} %get-tuple-element.666, s32[]{:T(128)} %get-tuple-element.665, bf16[12288,384]{1,0:T(8,128)(2,1)} %get-tuple-element.695, f32[256]{0:T(256)S(1)} %bitcast.268, s32[256]{0:T(256)S(1)} %bitcast.284, f32[256]{0:T(256)S(1)} %bitcast.254, s32[256]{0:T(256)S(1)} %bitcast.270, ...), kind=kOutput, calls=%fused_computation.56.clone.1 | convolution fusion | flops 2566914048 | bytes 9863680 | tf_op jit(solution)/shard_map/while/body/eval_jaxpr/dot_general | solution.py:67
  376.5 66.2 %while.25 = (s32[]{:T(128)}, f32[3,1536,128]{1,2,0:T(8,128)}, s32[3]{0:T(128)S(1)}, s32[16,384]{1,0:T(8,128)}, f32[16,384]{1,0:T(8,128)}, /*index=5*/bf16[1536,6...) while((s32[]{:T(128)}, f32[3,1536,128]{1,2,0:T(8,128)}, ...), condition=%wide.region_7.8_spmd.clone.clone, body=%wide.region_6.7_spmd.clone.clone.sunk | while | flops 2453667840 | bytes 19711052 | solution.py:82
  378.9 1.1 fusion.162
  380.0 18.5 %fusion.163 = f32[3,1536,128]{1,2,0:T(8,128)} fusion(f32[3,1536,128]{1,2,0:T(8,128)} %get-tuple-element.591, s32[]{:T(128)} %get-tuple-element.590, bf16[1536,6144]{1,0:T(8,128)(2,1)} %get-tuple-element.620, f32[128]{0:T(128)S(1)} %get-tuple-element.533, s32[128]{0:T(128)S(1)} %get-tuple-element.534, f32[128]{0:T(128)S(1)} %get-tuple-element.535, ...), kind=kOutput, calls=%fused_computation.78.clone.1 | convolution fusion | flops 2453667840 | bytes 19677696 | tf_op jit(solution)/shard_map/while/body/eval_jaxpr/dot_general | solution.py:78
  402.1 18.5 %fusion.163 = f32[3,1536,128]{1,2,0:T(8,128)} fusion(f32[3,1536,128]{1,2,0:T(8,128)} %get-tuple-element.591, s32[]{:T(128)} %get-tuple-element.590, bf16[1536,6144]{1,0:T(8,128)(2,1)} %get-tuple-element.620, f32[128]{0:T(128)S(1)} %get-tuple-element.533, s32[128]{0:T(128)S(1)} %get-tuple-element.534, f32[128]{0:T(128)S(1)} %get-tuple-element.535, ...), kind=kOutput, calls=%fused_computation.78.clone.1 | convolution fusion | flops 2453667840 | bytes 19677696 | tf_op jit(solution)/shard_map/while/body/eval_jaxpr/dot_general | solution.py:78
  424.1 18.5 %fusion.163 = f32[3,1536,128]{1,2,0:T(8,128)} fusion(f32[3,1536,128]{1,2,0:T(8,128)} %get-tuple-element.591, s32[]{:T(128)} %get-tuple-element.590, bf16[1536,6144]{1,0:T(8,128)(2,1)} %get-tuple-element.620, f32[128]{0:T(128)S(1)} %get-tuple-element.533, s32[128]{0:T(128)S(1)} %get-tuple-element.534, f32[128]{0:T(128)S(1)} %get-tuple-element.535, ...), kind=kOutput, calls=%fused_computation.78.clone.1 | convolution fusion | flops 2453667840 | bytes 19677696 | tf_op jit(solution)/shard_map/while/body/eval_jaxpr/dot_general | solution.py:78
  442.7 2.1 copy.28
  444.8 3.8 fusion.79
  448.6 2.5 reshape.133
  451.1 31.9 %all_to_all.11 = bf16[128,18,256]{2,1,0:T(8,128)(2,1)S(1)} all-to-all(bf16[128,18,256]{2,1,0:T(8,128)(2,1)S(1)} %reshape.133), channel_id=1, replica_groups=mesh['alpha'=8,'beta'=16] {'alpha','beta'}, dimensions={0} | all-to-all | bytes 2359296 | tf_op jit(solution)/shard_map/all_to_all | solution.py:135
  483.4 4.2 gather_fusion
  491.2 63.8 %all-reduce = (f32[]{:T(128)}, f32[]{:T(128)}) all-reduce(f32[]{:T(128)} %get-tuple-element.261, f32[]{:T(128)} %get-tuple-element.260), channel_id=1, replica_groups=mesh['alpha'=8,'beta'=16] {'alpha','beta'}, use_global_device_ids=true, to_apply=%region_9.10 | all-reduce | flops 2 | bytes 16 | tf_op jit(solution)/shard_map/psum | solution.py:147
  556.4 1.3 multiply_reduce_fusion
  557.7 62.8 %psum.23 = f32[]{:T(128)} all-reduce(f32[]{:T(128)} %get-tuple-element.290), channel_id=1, replica_groups=mesh['alpha'=8,'beta'=16] {'alpha','beta'}, use_global_device_ids=true, to_apply=%region_13.14 | all-reduce | flops 1 | bytes 8 | tf_op jit(solution)/shard_map/psum | solution.py:150
  (98 shorter events, 24.9 us)
Async XLA Ops:
  7.2 3.7 copy-start.2
  7.2 5.3 copy-start.4
  7.2 135.9 %all-gather.3.cloned.1.call-start = ((), (), s32[]{:S(2)}) async-start(), calls=%async_computation.2 | async-start | bytes 10616832 | tf_op jit(solution)/shard_map/all_gather | solution.py:122
  8.0 6.2 copy-start.14
  8.0 6.2 copy-start.16
  8.0 6.2 copy-start.18
  8.0 6.2 copy-start.12
  8.0 7.0 %copy-start.10 = (pred[768]{0:T(1024)(128)(4,1)}, pred[768]{0:T(1024)(128)(4,1)S(1)}, u32[]{:S(2)}) copy-start(pred[768]{0:T(1024)(128)(4,1)S(1)} %get-tuple-element.361) | copy-start | bytes 2308
  8.0 7.8 %copy-start.8 = (pred[768]{0:T(1024)(128)(4,1)}, pred[768]{0:T(1024)(128)(4,1)S(1)}, u32[]{:S(2)}) copy-start(pred[768]{0:T(1024)(128)(4,1)S(1)} %get-tuple-element.356) | copy-start | bytes 2308
  90.4 2.5 copy-start.7
  90.4 2.5 copy-start.21
  90.4 3.1 copy-start.6
  90.4 3.1 copy-start.20
  92.1 284.3 %all-gather.5.cloned.1.call-start = ((), (), s32[]{:S(2)}) async-start(), calls=%async_computation.3 | async-start | bytes 20054016 | tf_op jit(solution)/shard_map/all_gather | solution.py:130
  442.7 2.1 copy-start.1
  451.1 32.2 %copy-start = (s32[768]{0:T(1024)S(1)}, s32[768]{0:T(1024)}, u32[]{:S(2)}) copy-start(s32[768]{0:T(1024)} %get-tuple-element.262) | copy-start | bytes 9220
  483.1 4.5 copy-start.5
  483.1 4.6 copy-start.19
  483.1 5.1 copy-start.17
  483.3 5.3 copy-start.15
  483.3 5.8 copy-start.13
  483.4 6.3 copy-start.11
  483.4 6.8 %copy-start.3 = (f32[42,768]{1,0:T(8,128)S(1)}, f32[42,768]{1,0:T(8,128)}, u32[]{:S(2)}) copy-start(f32[42,768]{1,0:T(8,128)} %param.15) | copy-start | bytes 387076
  483.4 6.8 %copy-start.9 = (pred[768]{0:T(1024)(128)(4,1)S(1)}, pred[768]{0:T(1024)(128)(4,1)}, u32[]{:S(2)}) copy-start(pred[768]{0:T(1024)(128)(4,1)} %copy-done.8) | copy-start | bytes 2308
Sparse Core Ops, SparseCore 0:
  92.2 50.7 all-gather.2
  145.2 129.1 all-gather.4
where the time goes:
time: 637 us; the launch traced here: 629 us
  matrix products  254 us (40%)
  blocking collectives  194 us (30%)
  local copies, waits for them, and re-layouts  70.9 us (11%)
  waiting for transfers between devices  50.3 us (8%)
  loops' own time  33.5 us (5%)
  between operations  17.9 us (3%)
  other arithmetic  9.02 us (1%)
    dot_general x6, matrix products, alpha_one_block(): return jnp.dot(coupling, gathered, preferred_element_type=jnp.float32)  189 us
    psum x1, blocking collectives, body(): square_sum, cross_sum = lax.psum((own_square, own_cross), ('alpha', 'beta'))  63.8 us
    psum x1, blocking collectives, body(): residual_square = lax.psum(jnp.sum(residual * residual), ('alpha', 'beta'))  62.8 us
    dot_general x3, matrix products, beta_one_block(): lax.dot_general(gathered, coupling, (((1,), (1,)), ((), ())), preferred_e...  55.6 us
    all_gather x1, waiting for transfers between devices, body(): lax.all_gather(amplitude, 'alpha', axis=0, tiled=True)  49.5 us
    scatter x2, local copies, waits for them, and re-layouts, body(): outgoing = jnp.zeros((devices, capacity, det_width), jnp.bfloat16).at[tar...  38.3 us
    all_to_all x1, blocking collectives, body(): lax.all_to_all(outgoing, ('alpha', 'beta'), split_axis=0, concat_axis=0,...  35.2 us
    all_to_all x1, blocking collectives, body(): lax.all_to_all(sigma_grid.reshape(devices, capacity, det_width), ('alpha'...  31.9 us
  transfers between devices with their start and end apart: 2, of which 1 were waited for; matrix products, arithmetic and copies ran while one was open for 32% of the time, Pallas kernels for 0%

commit v1 on v0

--- a/solution.py
+++ b/solution.py
@@ -119,7 +119,9 @@
         alpha_weights,
         math.gcd(rows_alpha, 256),
         jnp.zeros((rows_alpha, cols_beta), jnp.float32),
-        lax.all_gather(amplitude, "alpha", axis=0, tiled=True),
+        jnp.concatenate(
+            lax.all_to_all(jnp.stack([amplitude] * lax.axis_size("alpha")), "alpha", 0, 0), axis=0
+        ),
     )
     beta_weights = live_weights(beta_values, beta_counts)
     beta_term = beta_fold(

time: 637 us -> 697 us (1.094)
  waiting for transfers between devices: 50.3 us -> 104 us
    all_to_all x0 -> x1, waiting for transfers between devices: none -> 104 us  [body(): lax.all_to_all(jnp.stack([amplitude] * lax.axis_size('alpha')), 'alpha',...]
    all_gather x1 -> x0, waiting for transfers between devices: 49.5 us -> none  [body(): lax.all_gather(amplitude, 'alpha', axis=0, tiled=True)]
  transfers between devices with their start and end apart: 2 -> 2, of which waited for: 1 -> 1; matrix products, arithmetic and copies ran while one was open for 32% -> 29% of each run, Pallas kernels for 0% -> 0%
where the time goes in v1:
time: 697 us; the launch traced here: 688 us
  matrix products  254 us (36%)
  blocking collectives  190 us (27%)
  waiting for transfers between devices  104 us (15%)
  local copies, waits for them, and re-layouts  73.9 us (11%)
  loops' own time  33.1 us (5%)
  between operations  17.9 us (3%)
  other arithmetic  9 us (1%)
    dot_general x6, matrix products, alpha_one_block(): return jnp.dot(coupling, gathered, preferred_element_type=jnp.float32)  189 us
    all_to_all x1, waiting for transfers between devices, body(): lax.all_to_all(jnp.stack([amplitude] * lax.axis_size('alpha')), 'alpha',...  104 us
    psum x1, blocking collectives, body(): square_sum, cross_sum = lax.psum((own_square, own_cross), ('alpha', 'beta'))  63.8 us
    psum x1, blocking collectives, body(): residual_square = lax.psum(jnp.sum(residual * residual), ('alpha', 'beta'))  62.8 us
    dot_general x3, matrix products, beta_one_block(): lax.dot_general(gathered, coupling, (((1,), (1,)), ((), ())), preferred_e...  55.6 us
    scatter x2, local copies, waits for them, and re-layouts, body(): outgoing = jnp.zeros((devices, capacity, det_width), jnp.bfloat16).at[tar...  38.3 us
    all_to_all x1, blocking collectives, body(): lax.all_to_all(outgoing, ('alpha', 'beta'), split_axis=0, concat_axis=0,...  35.2 us
    another operation x1, loops' own time, alpha_fold(): lax.map(alpha_one_block, jnp.arange(summed.shape[0] // block_rows, dtype=...  31.2 us
  transfers between devices with their start and end apart: 2, of which 1 were waited for; matrix products, arithmetic and copies ran while one was open for 29% of the time, Pallas kernels for 0%

profile of v1, /device:TPU:1, one launch (start us, length us, event | category | flops | bytes accessed | tf_op | source)
XLA Modules:
  0.0 688.5 jit_solution(11514088856719967041)
XLA Ops:
  8.7 1.3 fusion.143
  10.8 1.6 fusion.97
  16.8 37.6 %scatter_fusion = bf16[128,18,256]{2,0,1:T(8,128)(2,1)S(1)} fusion(bf16[128,18,256]{2,0,1:T(8,128)(2,1)S(1)} %broadcast_in_dim.410, s32[768]{0:T(1024)S(1)} %get-tuple-element.263, bf16[768,256]{1,0:T(8,128)(2,1)S(1)} %fusion.80), kind=kCustom, calls=%fused_computation.1 | custom fusion | bytes 1185792 | tf_op jit(solution)/shard_map/scatter | solution.py:112
  55.1 35.2 %all_to_all.15 = bf16[128,18,256]{2,1,0:T(8,128)(2,1)S(1)} all-to-all(bf16[128,18,256]{2,1,0:T(8,128)(2,1)S(1)} %copy.27), channel_id=1, replica_groups=mesh['alpha'=8,'beta'=16] {'alpha','beta'}, dimensions={0} | all-to-all | bytes 2359296 | tf_op jit(solution)/shard_map/all_to_all | solution.py:114
  91.2 4.5 stack.3
  95.7 6.7 all-to-all-start.1
  103.7 103.6 %all-to-all-done.1 = bf16[8,1536,384]{2,1,0:T(8,128)(2,1)} async-done(((bf16[8,1536,384]{2,1,0:T(8,128)(2,1)}), bf16[8,1536,384]{2,1,0:T(8,128)(2,1)}, u32[]{:S(2)}, u32[]{:S(2)}) %all-to-all-start.1) | async-done | bytes 9437216 | tf_op jit(solution)/shard_map/all_to_all | solution.py:123
  207.3 232.0 %while.24 = (s32[]{:T(128)}, f32[6,256,384]{2,1,0:T(8,128)}, s32[6]{0:T(128)S(1)}, s32[16,1536]{1,0:T(8,128)}, f32[16,1536]{1,0:T(8,128)S(1)}, /*index=5*/bf16[1...) while((s32[]{:T(128)}, f32[6,256,384]{2,1,0:T(8,128)}, ...), condition=%wide.region_5.6_spmd.clone.clone, body=%wide.region_4.5_spmd.clone.clone.sunk | while | flops 2566914048 | bytes 9929303 | solution.py:69
  227.7 1.3 constant_dynamic-slice_fusion.7
  229.0 31.5 %fusion.159 = f32[6,256,384]{2,1,0:T(8,128)} fusion(f32[6,256,384]{2,1,0:T(8,128)} %get-tuple-element.666, s32[]{:T(128)S(6)} %copy.41, bf16[12288,384]{1,0:T(8,128)(2,1)} %get-tuple-element.695, f32[256]{0:T(256)S(1)} %bitcast.269, s32[256]{0:T(256)S(1)} %bitcast.285, f32[256]{0:T(256)S(1)} %bitcast.255, s32[256]{0:T(256)S(1)} %bitcast.271, ...), kind=kOutput, calls=%fused_computation.56.clone.1 | convolution fusion | flops 2566914048 | bytes 9863172 | tf_op jit(solution)/shard_map/while/body/eval_jaxpr/dot_general | solution.py:67
  261.9 1.4 constant_dynamic-slice_fusion.7
  263.3 31.4 %fusion.159 = f32[6,256,384]{2,1,0:T(8,128)} fusion(f32[6,256,384]{2,1,0:T(8,128)} %get-tuple-element.666, s32[]{:T(128)S(6)} %copy.41, bf16[12288,384]{1,0:T(8,128)(2,1)} %get-tuple-element.695, f32[256]{0:T(256)S(1)} %bitcast.269, s32[256]{0:T(256)S(1)} %bitcast.285, f32[256]{0:T(256)S(1)} %bitcast.255, s32[256]{0:T(256)S(1)} %bitcast.271, ...), kind=kOutput, calls=%fused_computation.56.clone.1 | convolution fusion | flops 2566914048 | bytes 9863172 | tf_op jit(solution)/shard_map/while/body/eval_jaxpr/dot_general | solution.py:67
  296.1 1.2 constant_dynamic-slice_fusion.7
  297.3 31.5 %fusion.159 = f32[6,256,384]{2,1,0:T(8,128)} fusion(f32[6,256,384]{2,1,0:T(8,128)} %get-tuple-element.666, s32[]{:T(128)S(6)} %copy.41, bf16[12288,384]{1,0:T(8,128)(2,1)} %get-tuple-element.695, f32[256]{0:T(256)S(1)} %bitcast.269, s32[256]{0:T(256)S(1)} %bitcast.285, f32[256]{0:T(256)S(1)} %bitcast.255, s32[256]{0:T(256)S(1)} %bitcast.271, ...), kind=kOutput, calls=%fused_computation.56.clone.1 | convolution fusion | flops 2566914048 | bytes 9863172 | tf_op jit(solution)/shard_map/while/body/eval_jaxpr/dot_general | solution.py:67
  330.1 1.2 constant_dynamic-slice_fusion.7
  331.3 31.4 %fusion.159 = f32[6,256,384]{2,1,0:T(8,128)} fusion(f32[6,256,384]{2,1,0:T(8,128)} %get-tuple-element.666, s32[]{:T(128)S(6)} %copy.41, bf16[12288,384]{1,0:T(8,128)(2,1)} %get-tuple-element.695, f32[256]{0:T(256)S(1)} %bitcast.269, s32[256]{0:T(256)S(1)} %bitcast.285, f32[256]{0:T(256)S(1)} %bitcast.255, s32[256]{0:T(256)S(1)} %bitcast.271, ...), kind=kOutput, calls=%fused_computation.56.clone.1 | convolution fusion | flops 2566914048 | bytes 9863172 | tf_op jit(solution)/shard_map/while/body/eval_jaxpr/dot_general | solution.py:67
  364.1 1.4 constant_dynamic-slice_fusion.7
  365.5 31.5 %fusion.159 = f32[6,256,384]{2,1,0:T(8,128)} fusion(f32[6,256,384]{2,1,0:T(8,128)} %get-tuple-element.666, s32[]{:T(128)S(6)} %copy.41, bf16[12288,384]{1,0:T(8,128)(2,1)} %get-tuple-element.695, f32[256]{0:T(256)S(1)} %bitcast.269, s32[256]{0:T(256)S(1)} %bitcast.285, f32[256]{0:T(256)S(1)} %bitcast.255, s32[256]{0:T(256)S(1)} %bitcast.271, ...), kind=kOutput, calls=%fused_computation.56.clone.1 | convolution fusion | flops 2566914048 | bytes 9863172 | tf_op jit(solution)/shard_map/while/body/eval_jaxpr/dot_general | solution.py:67
  398.3 1.2 constant_dynamic-slice_fusion.7
  399.5 31.5 %fusion.159 = f32[6,256,384]{2,1,0:T(8,128)} fusion(f32[6,256,384]{2,1,0:T(8,128)} %get-tuple-element.666, s32[]{:T(128)S(6)} %copy.41, bf16[12288,384]{1,0:T(8,128)(2,1)} %get-tuple-element.695, f32[256]{0:T(256)S(1)} %bitcast.269, s32[256]{0:T(256)S(1)} %bitcast.285, f32[256]{0:T(256)S(1)} %bitcast.255, s32[256]{0:T(256)S(1)} %bitcast.271, ...), kind=kOutput, calls=%fused_computation.56.clone.1 | convolution fusion | flops 2566914048 | bytes 9863172 | tf_op jit(solution)/shard_map/while/body/eval_jaxpr/dot_general | solution.py:67
  439.4 66.2 %while.25 = (s32[]{:T(128)}, f32[3,1536,128]{1,2,0:T(8,128)}, s32[3]{0:T(128)S(1)}, s32[16,384]{1,0:T(8,128)}, f32[16,384]{1,0:T(8,128)}, /*index=5*/bf16[1536,6...) while((s32[]{:T(128)}, f32[3,1536,128]{1,2,0:T(8,128)}, ...), condition=%wide.region_7.8_spmd.clone.clone, body=%wide.region_6.7_spmd.clone.clone.sunk | while | flops 2453667840 | bytes 19710552 | solution.py:82
  442.9 18.5 %fusion.163 = f32[3,1536,128]{1,2,0:T(8,128)} fusion(f32[3,1536,128]{1,2,0:T(8,128)} %get-tuple-element.591, s32[]{:T(128)S(6)} %copy.35, bf16[1536,6144]{1,0:T(8,128)(2,1)} %get-tuple-element.620, f32[128]{0:T(128)S(1)} %get-tuple-element.533, s32[128]{0:T(128)S(1)} %get-tuple-element.534, f32[128]{0:T(128)S(1)} %get-tuple-element.535, ...), kind=kOutput, calls=%fused_computation.78.clone.1 | convolution fusion | flops 2453667840 | bytes 19677188 | tf_op jit(solution)/shard_map/while/body/eval_jaxpr/dot_general | solution.py:78
  465.0 18.5 %fusion.163 = f32[3,1536,128]{1,2,0:T(8,128)} fusion(f32[3,1536,128]{1,2,0:T(8,128)} %get-tuple-element.591, s32[]{:T(128)S(6)} %copy.35, bf16[1536,6144]{1,0:T(8,128)(2,1)} %get-tuple-element.620, f32[128]{0:T(128)S(1)} %get-tuple-element.533, s32[128]{0:T(128)S(1)} %get-tuple-element.534, f32[128]{0:T(128)S(1)} %get-tuple-element.535, ...), kind=kOutput, calls=%fused_computation.78.clone.1 | convolution fusion | flops 2453667840 | bytes 19677188 | tf_op jit(solution)/shard_map/while/body/eval_jaxpr/dot_general | solution.py:78
  487.0 18.5 %fusion.163 = f32[3,1536,128]{1,2,0:T(8,128)} fusion(f32[3,1536,128]{1,2,0:T(8,128)} %get-tuple-element.591, s32[]{:T(128)S(6)} %copy.35, bf16[1536,6144]{1,0:T(8,128)(2,1)} %get-tuple-element.620, f32[128]{0:T(128)S(1)} %get-tuple-element.533, s32[128]{0:T(128)S(1)} %get-tuple-element.534, f32[128]{0:T(128)S(1)} %get-tuple-element.535, ...), kind=kOutput, calls=%fused_computation.78.clone.1 | convolution fusion | flops 2453667840 | bytes 19677188 | tf_op jit(solution)/shard_map/while/body/eval_jaxpr/dot_general | solution.py:78
  505.6 2.1 copy.28
  507.7 3.8 fusion.79
  511.5 2.5 reshape.136
  514.0 28.1 %all_to_all.16 = bf16[128,18,256]{2,1,0:T(8,128)(2,1)S(1)} all-to-all(bf16[128,18,256]{2,1,0:T(8,128)(2,1)S(1)} %reshape.136), channel_id=1, replica_groups=mesh['alpha'=8,'beta'=16] {'alpha','beta'}, dimensions={0} | all-to-all | bytes 2359296 | tf_op jit(solution)/shard_map/all_to_all | solution.py:137
  542.4 4.2 gather_fusion
  550.3 63.8 %all-reduce = (f32[]{:T(128)}, f32[]{:T(128)}) all-reduce(f32[]{:T(128)} %get-tuple-element.261, f32[]{:T(128)} %get-tuple-element.260), channel_id=1, replica_groups=mesh['alpha'=8,'beta'=16] {'alpha','beta'}, use_global_device_ids=true, to_apply=%region_9.10 | all-reduce | flops 2 | bytes 16 | tf_op jit(solution)/shard_map/psum | solution.py:149
  615.4 1.3 multiply_reduce_fusion
  616.7 62.8 %psum.23 = f32[]{:T(128)} all-reduce(f32[]{:T(128)} %get-tuple-element.290), channel_id=1, replica_groups=mesh['alpha'=8,'beta'=16] {'alpha','beta'}, use_global_device_ids=true, to_apply=%region_13.14 | all-reduce | flops 1 | bytes 8 | tf_op jit(solution)/shard_map/psum | solution.py:152
  (100 shorter events, 26.5 us)
Async XLA Ops:
  7.2 3.6 copy-start.3
  7.2 5.2 copy-start.5
  10.7 4.2 copy-start.13
  10.7 4.2 copy-start.15
  10.7 4.2 copy-start.17
  10.7 4.2 copy-start.19
  10.7 4.2 copy-start.11
  10.8 5.0 copy-start.9
  91.2 4.5 copy-start.1
  95.7 7.4 %copy-start.8 = (bf16[16,384]{1,0:T(8,128)(2,1)S(1)}, bf16[16,384]{1,0:T(8,128)(2,1)}, u32[]{:S(2)}) copy-start(bf16[16,384]{1,0:T(8,128)(2,1)} %param.23) | copy-start | bytes 36868
  95.7 7.4 %copy-start.22 = (s32[384]{0:T(512)S(1)}, s32[384]{0:T(512)}, u32[]{:S(2)}) copy-start(s32[384]{0:T(512)} %param.24) | copy-start | bytes 4612
  95.7 8.0 %copy-start.7 = (bf16[16,1536]{1,0:T(8,128)(2,1)S(1)}, bf16[16,1536]{1,0:T(8,128)(2,1)}, u32[]{:S(2)}) copy-start(bf16[16,1536]{1,0:T(8,128)(2,1)} %param.20) | copy-start | bytes 147460
  95.7 8.0 %copy-start.21 = (s32[1536]{0:T(1024)S(1)}, s32[1536]{0:T(1024)}, u32[]{:S(2)}) copy-start(s32[1536]{0:T(1024)} %param.21) | copy-start | bytes 18436
  95.7 111.6 %all-to-all-start.1 = ((bf16[8,1536,384]{2,1,0:T(8,128)(2,1)}), bf16[8,1536,384]{2,1,0:T(8,128)(2,1)}, u32[]{:S(2)}, u32[]{:S(2)}) async-start(bf16[8,1536,384]{2,1,0:T(8,128)(2,1)} %stack.3), calls=%async_computation.1 | async-start | bytes 18874368 | tf_op jit(solution)/shard_map/all_to_all | solution.py:123
  102.4 337.0 %all-gather.2.cloned.1.call-start = ((), (), s32[]{:S(2)}) async-start(), calls=%async_computation.3 | async-start | bytes 20054016 | tf_op jit(solution)/shard_map/all_gather | solution.py:132
  505.6 2.1 copy-start.2
  514.0 28.4 %copy-start = (s32[768]{0:T(1024)S(1)}, s32[768]{0:T(1024)}, u32[]{:S(2)}) copy-start(s32[768]{0:T(1024)} %get-tuple-element.262) | copy-start | bytes 9220
  542.1 4.5 copy-start.6
  542.1 4.6 copy-start.20
  542.1 5.1 copy-start.18
  542.4 5.3 copy-start.16
  542.4 5.8 copy-start.14
  542.4 6.3 copy-start.12
  542.4 6.8 copy-start.4
  542.4 6.8 copy-start.10
Sparse Core Ops, SparseCore 0:
  105.3 126.2 all-gather.1
